TPU v7x, 32 devices: a whole 2x2x4 slice. The times are simulated.
32 devices in a mesh: row: 8 (over y, x, core), col: 4 (over z).
Axes of the slice: x: 2, y: 2, z: 4, core: 2. Of those that a mesh axis runs over, the one named last changes fastest.
Arguments:
- vectors: bfloat16 [32768, 64], P(('row', 'col')), may hold values from -6 to 6
- cotangent: bfloat16 [32768, 64], P(('row', 'col')), may hold values from -360 to 360, as said below
- gap_weights: float32 [64, 64], replicated, as said below
- row_tile: int32 [8, 4, 128], P('row', 'col'), may hold values from -1 to 31, as said below
- col_tile: int32 [8, 4, 128], P('row', 'col'), may hold values from -1 to 63, as said below
Outputs:
- tile_grads: bfloat16 [8, 4, 128, 128, 128], P('row', 'col')
Inputs may be any that keep to these rules, and one draw needn't show every extreme that they name: `cotangent`: fresh draw of one law: entries of order one times a row scale rising along the vertices and a column scale per eigenvector. `gap_weights`: Positive, within a factor of 5 of 0.00125 / sqrt(32768). Used slots come first in each cell and name distinct tiles there; row_tile and col_tile are -1 together in padding slots; some cell uses all 128 slots. `col_tile`: padding slots are -1, as in row_tile.
All inputs are finite; a program needn't handle non-finite values.
Results may differ from a plain program's by a relative error of at most 0.011.
Values may be sent and summed in bfloat16 or wider, within the bound.
No kernel may reach another device: no remote copies, remote signals or barrier semaphores. Data moves between devices by JAX's collectives and lax.ppermute only.
A program may use at most 64 MiB of HBM per device.

v0:
```python
import jax
import jax.numpy as jnp
from jax import lax
from jax.sharding import PartitionSpec as P


def split_scaled(scaled):
    scaled_hi = scaled.astype(jnp.bfloat16)
    scaled_lo = (scaled - scaled_hi.astype(jnp.float32)).astype(jnp.bfloat16)
    return (scaled_hi, scaled_lo)


def mixed_rows(vec_rows, halves):
    first = jnp.dot(vec_rows, halves[0], preferred_element_type=jnp.float32)
    second = jnp.dot(vec_rows, halves[1], preferred_element_type=jnp.float32)
    return (first + second).astype(jnp.bfloat16)


def body(vectors, cotangent, gap_weights, row_tile, col_tile):
    eig_count = vectors.shape[1]
    partial_gram = lax.dot_general(
        vectors, cotangent, (((0,), (0,)), ((), ())), preferred_element_type=jnp.float32
    )
    gram_total = lax.psum(partial_gram, ("row", "col"))
    halves = split_scaled(gap_weights * gram_total)
    packed = vectors.reshape(-1, 2 * eig_count)
    vec_rows = lax.all_gather(packed, "col", axis=0, tiled=True).reshape(-1, eig_count)
    row_all = jnp.concatenate([mixed_rows(vec_rows, halves), vec_rows], axis=1)
    vec_rows = lax.all_gather(packed, "row", axis=0, tiled=True).reshape(-1, eig_count)
    col_all = jnp.concatenate([vec_rows, mixed_rows(vec_rows, halves)], axis=1)
    side = 128
    row_blocks = row_all.reshape(-1, side, 2 * eig_count)
    col_blocks = col_all.reshape(-1, side, 2 * eig_count)
    slot_count = row_tile.shape[-1]
    rows_idx = row_tile.reshape(slot_count)
    cols_idx = col_tile.reshape(slot_count)
    left_blocks = jnp.take(row_blocks, jnp.maximum(rows_idx, 0), axis=0)
    right_blocks = jnp.take(col_blocks, jnp.maximum(cols_idx, 0), axis=0)
    product = jnp.einsum(
        "gik,gjk->gij", left_blocks, right_blocks, preferred_element_type=jnp.float32
    )
    kept_mask = (rows_idx >= 0)[:, None, None]
    tiles_out = jnp.where(kept_mask, product, 0.0).astype(jnp.bfloat16)
    return tiles_out.reshape(1, 1, slot_count, side, side)


def solution(mesh):
    return jax.shard_map(
        body,
        mesh=mesh,
        in_specs=(
            P(("row", "col"), None),
            P(("row", "col"), None),
            P(),
            P("row", "col", None),
            P("row", "col", None),
        ),
        out_specs=P("row", "col", None, None, None),
        check_vma=False,
    )
```

profile of v0, /device:TPU:0, one launch (start us, length us, event | category | flops | bytes accessed | tf_op | source)
XLA Modules:
  0.0 105.1 jit_solution(2647410268700761317)
XLA Ops:
  6.5 1.1 %copy.6 = bf16[1024,64]{1,0:T(8,128)(2,1)S(1)} copy(bf16[1024,64]{0,1:T(8,128)(2,1)} %param.5) | data formatting | bytes 262144 | tf_op args[0]
  7.7 0.0 copy-start.2
  7.7 0.8 reshape.73
  8.5 0.0 all-gather.2.cloned.1.call-update
  8.5 17.6 %all_gather.6 = bf16[2048,128]{1,0:T(8,128)(2,1)S(1)} all-gather(bf16[512,128]{1,0:T(8,128)(2,1)} %reshape.73), channel_id=1, replica_groups=mesh['row'=8,'col'=4] {'col'}, dimensions={0}, use_global_device_ids=true | all-gather | bytes 655360 | tf_op jit(solution)/shard_map/all_gather | solution.py:27
  26.1 0.4 reshape.74
  26.5 0.4 concatenate.17
  26.9 0.2 fusion.18
  27.1 40.9 %psum.7 = f32[64,64]{1,0:T(8,128)S(1)} all-reduce(f32[64,64]{1,0:T(8,128)S(1)} %fusion.18), channel_id=1, replica_groups=mesh['row'=8,'col'=4] {'row','col'}, use_global_device_ids=true, to_apply=%region_0.0 | all-reduce | flops 4096 | bytes 32768 | tf_op jit(solution)/shard_map/psum | solution.py:24
  68.1 0.5 fusion.17
  68.6 1.3 %fusion.3 = bf16[4096,64]{0,1:T(8,128)(2,1)} fusion(f32[64,4096]{1,0:T(8,128)S(1)} %fusion.17, bf16[64,64]{1,0:T(8,128)(2,1)S(1)} %subtract_convert_fusion, bf16[4096,64]{1,0:T(8,128)(2,1)S(1)} %reshape.74), kind=kOutput, calls=%fused_computation.8 | convolution fusion | flops 34078720 | bytes 2105344 | tf_op jit(solution)/shard_map/dot_general | solution.py:15
  69.9 1.5 %copy.9 = bf16[4096,64]{1,0:T(8,128)(2,1)S(1)} copy(bf16[4096,64]{0,1:T(8,128)(2,1)} %fusion.3) | data formatting | bytes 1048576 | tf_op jit(solution)/shard_map/concatenate | solution.py:28
  71.5 0.6 pad_maximum_fusion.1
  72.0 0.0 copy-start.5
  72.1 3.0 %gather_fusion = bf16[128,128,128]{2,1,0:T(8,128)(2,1)} fusion(bf16[32,128,128]{2,1,0:T(8,128)(2,1)S(1)} %pad_maximum_fusion.1, s32[1024]{0:T(1024)S(1)} %pad_clamp_fusion.1), kind=kCustom, calls=%fused_computation | custom fusion | bytes 8389120 | tf_op jit(solution)/shard_map/jit(_take)/gather | solution.py:37
  75.1 0.0 all-gather.2.cloned.1.call-done
  75.1 2.7 %reshape.75 = bf16[8192,64]{1,0:T(8,128)(2,1)S(1)} reshape(bf16[4096,128]{1,0:T(8,128)(2,1)} %all-gather.2.cloned.1.call-done) | data formatting | bytes 2097152 | tf_op jit(solution)/shard_map/reshape | solution.py:29
  77.9 0.9 fusion.16
  78.8 0.9 fusion.1
  79.7 1.8 %copy.10 = bf16[8192,64]{1,0:T(8,128)(2,1)} copy(bf16[8192,64]{0,1:T(8,128)(2,1)S(1)} %fusion.1) | data formatting | bytes 2097152 | tf_op jit(solution)/shard_map/concatenate | solution.py:30
  81.4 1.9 %concatenate.19 = bf16[64,128,64]{2,1,0:T(8,128)(2,1)} reshape(bf16[4096,128]{1,0:T(8,128)(2,1)S(1)} %copy-done.1) | data formatting | bytes 2097152 | tf_op jit(solution)/shard_map/concatenate | solution.py:30
  83.3 3.4 %pad_maximum_fusion = bf16[64,128,128]{2,1,0:T(8,128)(2,1)S(1)} fusion(bf16[64,128,64]{2,1,0:T(8,128)(2,1)} %bitcast.26, bf16[64,128,64]{2,1,0:T(8,128)(2,1)} %concatenate.19), kind=kLoop, calls=%fused_computation.15 | loop fusion | flops 4194304 | bytes 4194304 | tf_op jit(solution)/shard_map/concatenate | solution.py:30
  86.7 3.1 %gather_fusion.1 = bf16[128,128,128]{2,1,0:T(8,128)(2,1)} fusion(bf16[64,128,128]{2,1,0:T(8,128)(2,1)S(1)} %pad_maximum_fusion, s32[1024]{0:T(1024)S(1)} %pad_clamp_fusion), kind=kCustom, calls=%fused_computation.1 | custom fusion | bytes 8389120 | tf_op jit(solution)/shard_map/jit(_take)/gather | solution.py:38
  89.7 8.6 %fusion.4 = bf16[1,1,128,128,128]{4,3,2,1,0:T(8,128)(2,1)} fusion(pred[128]{0:T(512)(128)(4,1)S(1)} %get-tuple-element.6, bf16[128,128,128]{2,1,0:T(8,128)(2,1)} %gather_fusion.1, pred[128]{0:T(512)(128)(4,1)S(1)} %get-tuple-element.7, bf16[128,128,128]{2,1,0:T(8,128)(2,1)} %gather_fusion, pred[128]{0:T(512)(128)(4,1)S(1)} %get-tuple-element.5), kind=kOutput, calls=%fused_computation.9 | convolution fusion | flops 545259520 | bytes 12583296 | tf_op jit(solution)/shard_map/gik,gjk->gij/dot_general | solution.py:39
  (17 shorter events, 0.1 us)
Async XLA Ops:
  6.5 20.4 %copy-start = (bf16[1024,64]{0,1:T(8,128)(2,1)S(1)}, bf16[1024,64]{0,1:T(8,128)(2,1)}, u32[]{:S(2)}) copy-start(bf16[1024,64]{0,1:T(8,128)(2,1)} %param.6) | copy-start | bytes 393220
  6.5 68.6 %all-gather.2.cloned.1.call-start = ((), (), s32[]{:S(2)}) async-start(), calls=%async_computation | async-start | bytes 1179648 | tf_op jit(solution)/shard_map/all_gather | solution.py:29
  7.7 19.3 %copy-start.2 = (bf16[1024,64]{0,1:T(8,128)(2,1)S(1)}, bf16[1024,64]{0,1:T(8,128)(2,1)}, u32[]{:S(2)}) copy-start(bf16[1024,64]{0,1:T(8,128)(2,1)} %param.5) | copy-start | bytes 393220
  8.5 59.6 %copy-start.3 = (f32[64,64]{1,0:T(8,128)S(1)}, f32[64,64]{1,0:T(8,128)}, u32[]{:S(2)}) copy-start(f32[64,64]{1,0:T(8,128)} %param.7) | copy-start | bytes 49156
  68.6 2.8 %copy-start.4 = (s32[1,1,128]{2,1,0:T(1,128)S(1)}, s32[1,1,128]{2,1,0:T(1,128)}, u32[]{:S(2)}) copy-start(s32[1,1,128]{2,1,0:T(1,128)} %param.8) | copy-start | bytes 1540
  72.0 3.0 %copy-start.5 = (s32[1,1,128]{2,1,0:T(1,128)S(1)}, s32[1,1,128]{2,1,0:T(1,128)}, u32[]{:S(2)}) copy-start(s32[1,1,128]{2,1,0:T(1,128)} %param.9) | copy-start | bytes 1540
  79.7 1.8 %copy-start.1 = (bf16[4096,128]{1,0:T(8,128)(2,1)S(1)}, bf16[4096,128]{1,0:T(8,128)(2,1)}, u32[]{:S(2)}) copy-start(bf16[4096,128]{1,0:T(8,128)(2,1)} %all-gather.2.cloned.1.call-done) | copy-start | bytes 3145732
Sparse Core Ops, SparseCore 0:
  9.2 26.1 all-gather.1
where the time goes:
time: 105 us
  blocking collectives  58.5 us (56%)
  local copies, waits for them, and re-layouts  16.7 us (16%)
  between operations  13.6 us (13%)
  matrix products  12.3 us (12%)
  other arithmetic  4 us (4%)
    psum x1, blocking collectives, body(): gram_total = lax.psum(partial_gram, ('row', 'col'))  40.9 us
    all_gather x1, blocking collectives, body(): lax.all_gather(packed, 'col', axis=0, tiled=True).reshape(-1, eig_count)  17.6 us
    dot_general x1, matrix products, body(): jnp.einsum('gik,gjk->gij', left_blocks, right_blocks, preferred_element_t...  8.57 us
    concatenate x2, local copies, waits for them, and re-layouts, body(): col_all = jnp.concatenate([vec_rows, mixed_rows(vec_rows, halves)], axis=1)  3.61 us
    concatenate x1, other arithmetic, body(): col_all = jnp.concatenate([vec_rows, mixed_rows(vec_rows, halves)], axis=1)  3.37 us
    gather x1, local copies, waits for them, and re-layouts, body(): right_blocks = jnp.take(col_blocks, jnp.maximum(cols_idx, 0), axis=0)  3.07 us
    gather x1, local copies, waits for them, and re-layouts, body(): left_blocks = jnp.take(row_blocks, jnp.maximum(rows_idx, 0), axis=0)  3.03 us
    reshape x1, local copies, waits for them, and re-layouts, body(): lax.all_gather(packed, 'row', axis=0, tiled=True).reshape(-1, eig_count)  2.75 us
  transfers between devices with their start and end apart: 1, of which 0 were waited for; matrix products, arithmetic and copies ran while one was open for 8% of the time, Pallas kernels for 0%

commit v1 on v0

v1 whole, which is shorter than its diff:
```python
import functools

import jax
import jax.numpy as jnp
from jax import lax
from jax.experimental import pallas as pl
from jax.experimental.pallas import tpu as pltpu
from jax.sharding import PartitionSpec as P

SIDE = 128


def swap(value, axis, step, size):
    return lax.ppermute(value, axis, [(i, i ^ step) for i in range(size)])


def total_over(value, axis, size):
    if size & (size - 1):
        return lax.psum(value, axis)
    step = 1
    while step < size:
        value = value + swap(value, axis, step, size)
        step *= 2
    return value


def tiles_kernel(row_count, col_count, row_idx, col_idx, place, total_ref, *refs):
    row_parts = refs[:row_count]
    col_parts = refs[row_count : row_count + col_count]
    out_ref, left, right, tiles, sems = refs[row_count + col_count :]
    eigs, own = row_parts[0].shape
    per_dev = own // SIDE
    slots = out_ref.shape[0]
    total = total_ref[...]
    high = total.astype(jnp.bfloat16)
    low = (total - high.astype(jnp.float32)).astype(jnp.bfloat16)
    for s in range(col_count):
        part = col_parts[s][...]
        for b in range(per_dev):
            right[s * per_dev + b] = part[:, b * SIDE : (b + 1) * SIDE]
    dims = (((0,), (0,)), ((), ()))
    for s in range(row_count):
        part = row_parts[s][...]
        mixed = lax.dot_general(part, high, dims, preferred_element_type=jnp.float32)
        mixed = mixed + lax.dot_general(part, low, dims, preferred_element_type=jnp.float32)
        left[s * per_dev : (s + 1) * per_dev] = mixed.astype(jnp.bfloat16).reshape(per_dev, SIDE, eigs)
    here_row = place[0]
    here_col = place[1]
    chunks = sems.shape[0]
    step = slots // chunks

    def copy(c):
        return pltpu.make_async_copy(
            tiles.at[pl.ds(c * step, step)], out_ref.at[pl.ds(c * step, step)], sems.at[c]
        )

    def chunk(c, carry):
        for t in range(step):
            g = c * step + t
            i = row_idx[g]
            j = col_idx[g]
            kept = i >= 0
            i = jnp.maximum(i, 0)
            j = jnp.maximum(j, 0)
            li = ((i // per_dev) ^ here_col) * per_dev + i % per_dev
            rj = ((j // per_dev) ^ here_row) * per_dev + j % per_dev
            tile = jnp.dot(left[li], right[rj], preferred_element_type=jnp.float32)
            tiles[g] = jnp.where(kept, tile, 0.0).astype(jnp.bfloat16)
        copy(c).start()
        return carry

    lax.fori_loop(0, chunks, chunk, 0)
    for c in range(chunks):
        copy(c).wait()


def body(row_size, col_size, vectors, cotangent, gap_weights, row_tile, col_tile):
    own, eigs = vectors.shape
    flat = vectors.T
    gram = lax.dot_general(flat, cotangent, (((1,), (0,)), ((), ())), preferred_element_type=jnp.float32)
    scaled = gap_weights * gram
    total = scaled + scaled.T
    row_parts = [flat] + [swap(flat, "col", s, col_size) for s in range(1, col_size)]
    col_parts = [flat] + [swap(flat, "row", s, row_size) for s in range(1, row_size)]
    total = total_over(total, "row", row_size)
    total = total_over(total, "col", col_size)
    slots = row_tile.shape[-1]
    per_dev = own // SIDE
    place = jnp.stack([lax.axis_index("row"), lax.axis_index("col")]).astype(jnp.int32)
    vmem = pl.BlockSpec(memory_space=pltpu.VMEM)
    smem = pl.BlockSpec(memory_space=pltpu.SMEM)
    chunks = 8 if slots % 8 == 0 else 1
    out = pl.pallas_call(
        functools.partial(tiles_kernel, col_size, row_size),
        out_shape=jax.ShapeDtypeStruct((slots, SIDE, SIDE), jnp.bfloat16),
        in_specs=[smem, smem, smem] + [vmem] * (1 + row_size + col_size),
        out_specs=pl.BlockSpec(memory_space=pl.ANY),
        scratch_shapes=[
            pltpu.VMEM((col_size * per_dev, SIDE, eigs), jnp.bfloat16),
            pltpu.VMEM((row_size * per_dev, eigs, SIDE), jnp.bfloat16),
            pltpu.VMEM((slots, SIDE, SIDE), jnp.bfloat16),
            pltpu.SemaphoreType.DMA((chunks,)),
        ],
    )(row_tile.reshape(slots), col_tile.reshape(slots), place, total, *row_parts, *col_parts)
    return out.reshape(1, 1, slots, SIDE, SIDE)


def solution(mesh):
    return jax.shard_map(
        functools.partial(body, mesh.shape["row"], mesh.shape["col"]),
        mesh=mesh,
        in_specs=(
            P(("row", "col"), None),
            P(("row", "col"), None),
            P(),
            P("row", "col", None),
            P("row", "col", None),
        ),
        out_specs=P("row", "col", None, None, None),
        check_vma=False,
    )
```

time: 105 us -> 53.5 us (0.51)
  blocking collectives: 58.5 us -> 0 us
  waiting for transfers between devices: 0.04 us -> 23.1 us
  starting transfers between devices: 0.01 us -> 20.5 us
  local copies, waits for them, and re-layouts: 16.7 us -> 1.66 us
  between operations: 13.6 us -> 0.11 us
  matrix products: 12.3 us -> 1.07 us
  Pallas kernels: 0 us -> 5.69 us
  other arithmetic: 4 us -> 1.25 us
    psum x1 -> x0, blocking collectives: 40.9 us -> none  [body(): gram_total = lax.psum(partial_gram, ('row', 'col'))]
    ppermute x0 -> x15, waiting for transfers between devices: none -> 23.1 us  [swap(): return lax.ppermute(value, axis, [(i, i ^ step) for i in range(size)])]
    ppermute x0 -> x15, starting transfers between devices: none -> 20.5 us  [swap(): return lax.ppermute(value, axis, [(i, i ^ step) for i in range(size)])]
    all_gather x1 -> x0, blocking collectives: 17.6 us -> none  [body(): lax.all_gather(packed, 'col', axis=0, tiled=True).reshape(-1, eig_count)]
    dot_general x6 -> x1, matrix products: 12.3 us -> 1.07 us  [body(): lax.dot_general(flat, cotangent, (((1,), (0,)), ((), ())), preferred_elem...]
    gather x2 -> x0, local copies, waits for them, and re-layouts: 6.1 us -> none  [the longest x1 3.07 us: body(): right_blocks = jnp.take(col_blocks, jnp.maximum(cols_idx, 0), axis=0)]
    pallas_call x0 -> x1, Pallas kernels: none -> 5.69 us  [body(): pl.pallas_call(functools.partial(tiles_kernel, col_size, row_size), out_s...]
    concatenate x4 -> x0, local copies, waits for them, and re-layouts: 5.53 us -> none  [the longest x2 3.61 us: body(): col_all = jnp.concatenate([vec_rows, mixed_rows(vec_rows, halves)], axis=1)]
  transfers between devices with their start and end apart: 1 -> 15, of which waited for: 0 -> 10; matrix products, arithmetic and copies ran while one was open for 8% -> 2% of each run, Pallas kernels for 0% -> 0%
where the time goes in v1:
time: 53.5 us; the launch traced here: 53.4 us
  waiting for transfers between devices  23.1 us (43%)
  starting transfers between devices  20.5 us (38%)
  Pallas kernels  5.69 us (11%)
  local copies, waits for them, and re-layouts  1.66 us (3%)
  other arithmetic  1.25 us (2%)
  matrix products  1.07 us (2%)
    ppermute x15, waiting for transfers between devices, swap(): return lax.ppermute(value, axis, [(i, i ^ step) for i in range(size)])  23.1 us
    ppermute x15, starting transfers between devices, swap(): return lax.ppermute(value, axis, [(i, i ^ step) for i in range(size)])  20.5 us
    pallas_call x1, Pallas kernels, body(): pl.pallas_call(functools.partial(tiles_kernel, col_size, row_size), out_s...  5.69 us
    unnamed x23, local copies, waits for them, and re-layouts  1.59 us
    dot_general x1, matrix products, body(): lax.dot_general(flat, cotangent, (((1,), (0,)), ((), ())), preferred_elem...  1.07 us
  transfers between devices with their start and end apart: 15, of which 10 were waited for; matrix products, arithmetic and copies ran while one was open for 2% of the time, Pallas kernels for 0%

profile of v1, /device:TPU:0, one launch (start us, length us, event | category | flops | bytes accessed | tf_op | source)
XLA Modules:
  0.0 53.4 jit_solution(880793813591704983)
XLA Ops:
  0.0 0.9 %copy.6 = f32[64,64]{0,1:T(8,128)S(1)} copy(f32[64,64]{1,0:T(8,128)} %param.7) | data formatting | bytes 32768 | tf_op args[2]
  0.9 1.1 %convolution_multiply_fusion = f32[64,64]{0,1:T(8,128)S(1)} fusion(f32[64,64]{0,1:T(8,128)S(1)} %copy.6, bf16[1024,64]{0,1:T(8,128)(2,1)} %param.5, bf16[1024,64]{0,1:T(8,128)(2,1)S(1)} %copy-done), kind=kOutput, calls=%fused_computation | convolution fusion | flops 8392704 | bytes 294912 | tf_op jit(solution)/shard_map/dot_general | solution.py:80
  2.7 0.9 %collective-permute-done = f32[64,64]{1,0:T(8,128)S(1)} collective-permute-done((f32[64,64]{1,0:T(8,128)S(1)}, f32[64,64]{1,0:T(8,128)S(1)}, u32[]{:S(2)}, u32[]{:S(2)}) %collective-permute-start) | collective-permute-done | bytes 16416 | tf_op jit(solution)/shard_map/ppermute | solution.py:14
  3.5 2.8 %collective-permute-start.1 = (f32[64,64]{1,0:T(8,128)S(1)}, f32[64,64]{1,0:T(8,128)S(1)}, u32[]{:S(2)}, u32[]{:S(2)}) collective-permute-start(f32[64,64]{1,0:T(8,128)S(1)} %add.19), channel_id=1, source_target_pairs={{0,8},{4,12},{8,0},{12,4},{16,24},{20,28},{24,16},{28,20},{1,9},{5... | collective-permute-start | bytes 49160 | tf_op jit(solution)/shard_map/ppermute | solution.py:14
  6.3 1.9 %collective-permute-done.1 = f32[64,64]{1,0:T(8,128)S(1)} collective-permute-done((f32[64,64]{1,0:T(8,128)S(1)}, f32[64,64]{1,0:T(8,128)S(1)}, u32[]{:S(2)}, u32[]{:S(2)}) %collective-permute-start.1) | collective-permute-done | bytes 16416 | tf_op jit(solution)/shard_map/ppermute | solution.py:14
  8.2 2.1 %collective-permute-start.2 = (f32[64,64]{1,0:T(8,128)S(1)}, f32[64,64]{1,0:T(8,128)S(1)}, u32[]{:S(2)}, u32[]{:S(2)}) collective-permute-start(f32[64,64]{1,0:T(8,128)S(1)} %add.20), channel_id=1, source_target_pairs={{0,16},{4,20},{8,24},{12,28},{16,0},{20,4},{24,8},{28,12},{1,17},{... | collective-permute-start | bytes 49160 | tf_op jit(solution)/shard_map/ppermute | solution.py:14
  10.3 1.9 %collective-permute-done.2 = f32[64,64]{1,0:T(8,128)S(1)} collective-permute-done((f32[64,64]{1,0:T(8,128)S(1)}, f32[64,64]{1,0:T(8,128)S(1)}, u32[]{:S(2)}, u32[]{:S(2)}) %collective-permute-start.2) | collective-permute-done | bytes 16416 | tf_op jit(solution)/shard_map/ppermute | solution.py:14
  12.2 2.1 %collective-permute-start.3 = (f32[64,64]{1,0:T(8,128)S(1)}, f32[64,64]{1,0:T(8,128)S(1)}, u32[]{:S(2)}, u32[]{:S(2)}) collective-permute-start(f32[64,64]{1,0:T(8,128)S(1)} %add.21), channel_id=1, source_target_pairs={{0,1},{1,0},{2,3},{3,2},{4,5},{5,4},{6,7},{7,6},{8,9},{9,8},{10,11... | collective-permute-start | bytes 49160 | tf_op jit(solution)/shard_map/ppermute | solution.py:14
  14.3 1.9 %collective-permute-done.3 = f32[64,64]{1,0:T(8,128)S(1)} collective-permute-done((f32[64,64]{1,0:T(8,128)S(1)}, f32[64,64]{1,0:T(8,128)S(1)}, u32[]{:S(2)}, u32[]{:S(2)}) %collective-permute-start.3) | collective-permute-done | bytes 16416 | tf_op jit(solution)/shard_map/ppermute | solution.py:14
  16.2 3.0 %collective-permute-start.4 = (f32[64,64]{1,0:T(8,128)S(1)}, f32[64,64]{1,0:T(8,128)S(1)}, u32[]{:S(2)}, u32[]{:S(2)}) collective-permute-start(f32[64,64]{1,0:T(8,128)S(1)} %add.22), channel_id=1, source_target_pairs={{0,2},{1,3},{2,0},{3,1},{4,6},{5,7},{6,4},{7,5},{8,10},{9,11},{10,... | collective-permute-start | bytes 49160 | tf_op jit(solution)/shard_map/ppermute | solution.py:14
  19.2 2.4 %collective-permute-start.13 = (bf16[64,1024]{1,0:T(8,128)(2,1)}, bf16[64,1024]{1,0:T(8,128)(2,1)S(1)}, u32[]{:S(2)}, u32[]{:S(2)}) collective-permute-start(bf16[64,1024]{1,0:T(8,128)(2,1)} %bitcast.11), channel_id=1, source_target_pairs={{0,24},{4,28},{8,16},{12,20},{16,8},{20,12},{24,0},{28,4},{1,25},{... | collective-permute-start | bytes 393224 | tf_op jit(solution)/shard_map/ppermute | solution.py:14
  21.7 1.4 %collective-permute-start.12 = (bf16[64,1024]{1,0:T(8,128)(2,1)}, bf16[64,1024]{1,0:T(8,128)(2,1)S(1)}, u32[]{:S(2)}, u32[]{:S(2)}) collective-permute-start(bf16[64,1024]{1,0:T(8,128)(2,1)} %bitcast.12), channel_id=1, source_target_pairs={{0,20},{4,16},{8,28},{12,24},{16,4},{20,0},{24,12},{28,8},{1,21},{... | collective-permute-start | bytes 393224 | tf_op jit(solution)/shard_map/ppermute | solution.py:14
  23.6 0.7 %collective-permute-start.10 = (bf16[64,1024]{1,0:T(8,128)(2,1)}, bf16[64,1024]{1,0:T(8,128)(2,1)S(1)}, u32[]{:S(2)}, u32[]{:S(2)}) collective-permute-start(bf16[64,1024]{1,0:T(8,128)(2,1)} %bitcast.14), channel_id=1, source_target_pairs={{0,12},{4,8},{8,4},{12,0},{16,28},{20,24},{24,20},{28,16},{1,13},{... | collective-permute-start | bytes 393224 | tf_op jit(solution)/shard_map/ppermute | solution.py:14
  24.3 1.8 %collective-permute-done.14.refs_11_ = bf16[64,1024]{1,0:T(8,128)(2,1)S(1)} collective-permute-done((bf16[64,1024]{1,0:T(8,128)(2,1)}, bf16[64,1024]{1,0:T(8,128)(2,1)S(1)}, u32[]{:S(2)}, u32[]{:S(2)}) %collective-permute-start.14) | collective-permute-done | bytes 131104 | tf_op jit(solution)/shard_map/ppermute | solution.py:14
  26.1 1.6 %collective-permute-start.9 = (bf16[64,1024]{1,0:T(8,128)(2,1)}, bf16[64,1024]{1,0:T(8,128)(2,1)S(1)}, u32[]{:S(2)}, u32[]{:S(2)}) collective-permute-start(bf16[64,1024]{1,0:T(8,128)(2,1)} %bitcast.15), channel_id=1, source_target_pairs={{0,8},{4,12},{8,0},{12,4},{16,24},{20,28},{24,16},{28,20},{1,9},{5... | collective-permute-start | bytes 393224 | tf_op jit(solution)/shard_map/ppermute | solution.py:14
  27.7 1.4 %collective-permute-done.13.refs_10_ = bf16[64,1024]{1,0:T(8,128)(2,1)S(1)} collective-permute-done((bf16[64,1024]{1,0:T(8,128)(2,1)}, bf16[64,1024]{1,0:T(8,128)(2,1)S(1)}, u32[]{:S(2)}, u32[]{:S(2)}) %collective-permute-start.13) | collective-permute-done | bytes 131104 | tf_op jit(solution)/shard_map/ppermute | solution.py:14
  29.1 2.6 %collective-permute-done.12.refs_9_ = bf16[64,1024]{1,0:T(8,128)(2,1)S(1)} collective-permute-done((bf16[64,1024]{1,0:T(8,128)(2,1)}, bf16[64,1024]{1,0:T(8,128)(2,1)S(1)}, u32[]{:S(2)}, u32[]{:S(2)}) %collective-permute-start.12) | collective-permute-done | bytes 131104 | tf_op jit(solution)/shard_map/ppermute | solution.py:14
  31.7 1.3 %collective-permute-start.7 = (bf16[64,1024]{1,0:T(8,128)(2,1)}, bf16[64,1024]{1,0:T(8,128)(2,1)S(1)}, u32[]{:S(2)}, u32[]{:S(2)}) collective-permute-start(bf16[64,1024]{1,0:T(8,128)(2,1)} %bitcast.17), channel_id=1, source_target_pairs={{0,3},{1,2},{2,1},{3,0},{4,7},{5,6},{6,5},{7,4},{8,11},{9,10},{10,... | collective-permute-start | bytes 393224 | tf_op jit(solution)/shard_map/ppermute | solution.py:14
  33.0 1.5 %collective-permute-done.11.refs_8_ = bf16[64,1024]{1,0:T(8,128)(2,1)S(1)} collective-permute-done((bf16[64,1024]{1,0:T(8,128)(2,1)}, bf16[64,1024]{1,0:T(8,128)(2,1)S(1)}, u32[]{:S(2)}, u32[]{:S(2)}) %collective-permute-start.11) | collective-permute-done | bytes 131104 | tf_op jit(solution)/shard_map/ppermute | solution.py:14
  34.7 1.7 %collective-permute-start.5 = (bf16[64,1024]{1,0:T(8,128)(2,1)}, bf16[64,1024]{1,0:T(8,128)(2,1)S(1)}, u32[]{:S(2)}, u32[]{:S(2)}) collective-permute-start(bf16[64,1024]{1,0:T(8,128)(2,1)} %bitcast.19), channel_id=1, source_target_pairs={{0,1},{1,0},{2,3},{3,2},{4,5},{5,4},{6,7},{7,6},{8,9},{9,8},{10,11... | collective-permute-start | bytes 393224 | tf_op jit(solution)/shard_map/ppermute | solution.py:14
  36.5 0.6 %pad_add_fusion.place = s32[2]{0:T(128)} fusion(s32[1]{0:T(128)} %bitcast.3, s32[1]{0:T(128)} %bitcast.2), kind=kLoop, calls=%fused_computation.2 | loop fusion | flops 2 | bytes 16 | tf_op jit(solution)/shard_map/stack | solution.py:89
  37.7 1.8 %collective-permute-done.7.refs_3_ = bf16[64,1024]{1,0:T(8,128)(2,1)S(1)} collective-permute-done((bf16[64,1024]{1,0:T(8,128)(2,1)}, bf16[64,1024]{1,0:T(8,128)(2,1)S(1)}, u32[]{:S(2)}, u32[]{:S(2)}) %collective-permute-start.7) | collective-permute-done | bytes 131104 | tf_op jit(solution)/shard_map/ppermute | solution.py:14
  39.5 7.4 %collective-permute-done.6.refs_2_ = bf16[64,1024]{1,0:T(8,128)(2,1)S(1)} collective-permute-done((bf16[64,1024]{1,0:T(8,128)(2,1)}, bf16[64,1024]{1,0:T(8,128)(2,1)S(1)}, u32[]{:S(2)}, u32[]{:S(2)}) %collective-permute-start.6) | collective-permute-done | bytes 131104 | tf_op jit(solution)/shard_map/ppermute | solution.py:14
  47.7 5.7 %shard_map.55 = bf16[128,128,128]{2,1,0:T(8,128)(2,1)} custom-call(s32[128]{0:T(128)} %bitcast.22, s32[128]{0:T(128)} %bitcast.23, s32[2]{0:T(128)} %pad_add_fusion.place, f32[64,64]{1,0:T(8,128)} %add.23.total_ref, bf16[64,1024]{1,0:T(8,128)(2,1)} %bitcast.20, bf16[64,1024]{1,0:T(8,128)(2,1)} %copy-done.10, bf16[64,1024]{1,0:T(8,128)(2,1)} %copy-done.9, ...), custom_call_target="tpu_custom_call" | custom-call | tf_op jit(solution)/shard_map/pallas_call | solution.py:93
  (39 shorter events, 2.7 us)
Async XLA Ops:
  0.0 0.9 %copy-start = (bf16[1024,64]{0,1:T(8,128)(2,1)S(1)}, bf16[1024,64]{0,1:T(8,128)(2,1)}, u32[]{:S(2)}) copy-start(bf16[1024,64]{0,1:T(8,128)(2,1)} %param.6) | copy-start | bytes 393220
  2.1 1.4 %collective-permute-start = (f32[64,64]{1,0:T(8,128)S(1)}, f32[64,64]{1,0:T(8,128)S(1)}, u32[]{:S(2)}, u32[]{:S(2)}) collective-permute-start(f32[64,64]{1,0:T(8,128)S(1)} %bitcast_add_fusion), channel_id=1, source_target_pairs={{0,4},{4,0},{8,12},{12,8},{16,20},{20,16},{24,28},{28,24},{1,5},{5... | collective-permute-start | bytes 49160 | tf_op jit(solution)/shard_map/ppermute | solution.py:14
  3.5 4.7 %collective-permute-start.1 = (f32[64,64]{1,0:T(8,128)S(1)}, f32[64,64]{1,0:T(8,128)S(1)}, u32[]{:S(2)}, u32[]{:S(2)}) collective-permute-start(f32[64,64]{1,0:T(8,128)S(1)} %add.19), channel_id=1, source_target_pairs={{0,8},{4,12},{8,0},{12,4},{16,24},{20,28},{24,16},{28,20},{1,9},{5... | collective-permute-start | bytes 49160 | tf_op jit(solution)/shard_map/ppermute | solution.py:14
  8.2 3.9 %collective-permute-start.2 = (f32[64,64]{1,0:T(8,128)S(1)}, f32[64,64]{1,0:T(8,128)S(1)}, u32[]{:S(2)}, u32[]{:S(2)}) collective-permute-start(f32[64,64]{1,0:T(8,128)S(1)} %add.20), channel_id=1, source_target_pairs={{0,16},{4,20},{8,24},{12,28},{16,0},{20,4},{24,8},{28,12},{1,17},{... | collective-permute-start | bytes 49160 | tf_op jit(solution)/shard_map/ppermute | solution.py:14
  12.2 4.0 %collective-permute-start.3 = (f32[64,64]{1,0:T(8,128)S(1)}, f32[64,64]{1,0:T(8,128)S(1)}, u32[]{:S(2)}, u32[]{:S(2)}) collective-permute-start(f32[64,64]{1,0:T(8,128)S(1)} %add.21), channel_id=1, source_target_pairs={{0,1},{1,0},{2,3},{3,2},{4,5},{5,4},{6,7},{7,6},{8,9},{9,8},{10,11... | collective-permute-start | bytes 49160 | tf_op jit(solution)/shard_map/ppermute | solution.py:14
  16.2 7.4 %collective-permute-start.4 = (f32[64,64]{1,0:T(8,128)S(1)}, f32[64,64]{1,0:T(8,128)S(1)}, u32[]{:S(2)}, u32[]{:S(2)}) collective-permute-start(f32[64,64]{1,0:T(8,128)S(1)} %add.22), channel_id=1, source_target_pairs={{0,2},{1,3},{2,0},{3,1},{4,6},{5,7},{6,4},{7,5},{8,10},{9,11},{10,... | collective-permute-start | bytes 49160 | tf_op jit(solution)/shard_map/ppermute | solution.py:14
  19.2 6.9 %collective-permute-start.14 = (bf16[64,1024]{1,0:T(8,128)(2,1)}, bf16[64,1024]{1,0:T(8,128)(2,1)S(1)}, u32[]{:S(2)}, u32[]{:S(2)}) collective-permute-start(bf16[64,1024]{1,0:T(8,128)(2,1)} %bitcast.10), channel_id=1, source_target_pairs={{0,28},{4,24},{8,20},{12,16},{16,12},{20,8},{24,4},{28,0},{1,29},{... | collective-permute-start | bytes 393224 | tf_op jit(solution)/shard_map/ppermute | solution.py:14
  19.2 9.9 %collective-permute-start.13 = (bf16[64,1024]{1,0:T(8,128)(2,1)}, bf16[64,1024]{1,0:T(8,128)(2,1)S(1)}, u32[]{:S(2)}, u32[]{:S(2)}) collective-permute-start(bf16[64,1024]{1,0:T(8,128)(2,1)} %bitcast.11), channel_id=1, source_target_pairs={{0,24},{4,28},{8,16},{12,20},{16,8},{20,12},{24,0},{28,4},{1,25},{... | collective-permute-start | bytes 393224 | tf_op jit(solution)/shard_map/ppermute | solution.py:14
  21.7 10.0 %collective-permute-start.12 = (bf16[64,1024]{1,0:T(8,128)(2,1)}, bf16[64,1024]{1,0:T(8,128)(2,1)S(1)}, u32[]{:S(2)}, u32[]{:S(2)}) collective-permute-start(bf16[64,1024]{1,0:T(8,128)(2,1)} %bitcast.12), channel_id=1, source_target_pairs={{0,20},{4,16},{8,28},{12,24},{16,4},{20,0},{24,12},{28,8},{1,21},{... | collective-permute-start | bytes 393224 | tf_op jit(solution)/shard_map/ppermute | solution.py:14
  23.1 11.4 %collective-permute-start.11 = (bf16[64,1024]{1,0:T(8,128)(2,1)}, bf16[64,1024]{1,0:T(8,128)(2,1)S(1)}, u32[]{:S(2)}, u32[]{:S(2)}) collective-permute-start(bf16[64,1024]{1,0:T(8,128)(2,1)} %bitcast.13), channel_id=1, source_target_pairs={{0,16},{4,20},{8,24},{12,28},{16,0},{20,4},{24,8},{28,12},{1,17},{... | collective-permute-start | bytes 393224 | tf_op jit(solution)/shard_map/ppermute | solution.py:14
  23.6 11.1 %collective-permute-start.10 = (bf16[64,1024]{1,0:T(8,128)(2,1)}, bf16[64,1024]{1,0:T(8,128)(2,1)S(1)}, u32[]{:S(2)}, u32[]{:S(2)}) collective-permute-start(bf16[64,1024]{1,0:T(8,128)(2,1)} %bitcast.14), channel_id=1, source_target_pairs={{0,12},{4,8},{8,4},{12,0},{16,28},{20,24},{24,20},{28,16},{1,13},{... | collective-permute-start | bytes 393224 | tf_op jit(solution)/shard_map/ppermute | solution.py:14
  26.1 20.8 %copy-start.1 = (bf16[64,1024]{1,0:T(8,128)(2,1)}, bf16[64,1024]{1,0:T(8,128)(2,1)S(1)}, u32[]{:S(2)}) copy-start(bf16[64,1024]{1,0:T(8,128)(2,1)S(1)} %collective-permute-done.14.refs_11_) | copy-start | bytes 393220
  26.1 11.6 %collective-permute-start.9 = (bf16[64,1024]{1,0:T(8,128)(2,1)}, bf16[64,1024]{1,0:T(8,128)(2,1)S(1)}, u32[]{:S(2)}, u32[]{:S(2)}) collective-permute-start(bf16[64,1024]{1,0:T(8,128)(2,1)} %bitcast.15), channel_id=1, source_target_pairs={{0,8},{4,12},{8,0},{12,4},{16,24},{20,28},{24,16},{28,20},{1,9},{5... | collective-permute-start | bytes 393224 | tf_op jit(solution)/shard_map/ppermute | solution.py:14
  29.1 17.9 %copy-start.2 = (bf16[64,1024]{1,0:T(8,128)(2,1)}, bf16[64,1024]{1,0:T(8,128)(2,1)S(1)}, u32[]{:S(2)}) copy-start(bf16[64,1024]{1,0:T(8,128)(2,1)S(1)} %collective-permute-done.13.refs_10_) | copy-start | bytes 393220
  29.1 8.6 %collective-permute-start.8 = (bf16[64,1024]{1,0:T(8,128)(2,1)}, bf16[64,1024]{1,0:T(8,128)(2,1)S(1)}, u32[]{:S(2)}, u32[]{:S(2)}) collective-permute-start(bf16[64,1024]{1,0:T(8,128)(2,1)} %bitcast.16), channel_id=1, source_target_pairs={{0,4},{4,0},{8,12},{12,8},{16,20},{20,16},{24,28},{28,24},{1,5},{5... | collective-permute-start | bytes 393224 | tf_op jit(solution)/shard_map/ppermute | solution.py:14
  31.7 15.3 %copy-start.3 = (bf16[64,1024]{1,0:T(8,128)(2,1)}, bf16[64,1024]{1,0:T(8,128)(2,1)S(1)}, u32[]{:S(2)}) copy-start(bf16[64,1024]{1,0:T(8,128)(2,1)S(1)} %collective-permute-done.12.refs_9_) | copy-start | bytes 393220
  31.7 7.8 %collective-permute-start.7 = (bf16[64,1024]{1,0:T(8,128)(2,1)}, bf16[64,1024]{1,0:T(8,128)(2,1)S(1)}, u32[]{:S(2)}, u32[]{:S(2)}) collective-permute-start(bf16[64,1024]{1,0:T(8,128)(2,1)} %bitcast.17), channel_id=1, source_target_pairs={{0,3},{1,2},{2,1},{3,0},{4,7},{5,6},{6,5},{7,4},{8,11},{9,10},{10,... | collective-permute-start | bytes 393224 | tf_op jit(solution)/shard_map/ppermute | solution.py:14
  34.5 12.4 %copy-start.4 = (bf16[64,1024]{1,0:T(8,128)(2,1)}, bf16[64,1024]{1,0:T(8,128)(2,1)S(1)}, u32[]{:S(2)}) copy-start(bf16[64,1024]{1,0:T(8,128)(2,1)S(1)} %collective-permute-done.11.refs_8_) | copy-start | bytes 393220
  34.5 12.4 %collective-permute-start.6 = (bf16[64,1024]{1,0:T(8,128)(2,1)}, bf16[64,1024]{1,0:T(8,128)(2,1)S(1)}, u32[]{:S(2)}, u32[]{:S(2)}) collective-permute-start(bf16[64,1024]{1,0:T(8,128)(2,1)} %bitcast.18), channel_id=1, source_target_pairs={{0,2},{1,3},{2,0},{3,1},{4,6},{5,7},{6,4},{7,5},{8,10},{9,11},{10,... | collective-permute-start | bytes 393224 | tf_op jit(solution)/shard_map/ppermute | solution.py:14
  34.7 12.2 %copy-start.5 = (bf16[64,1024]{1,0:T(8,128)(2,1)}, bf16[64,1024]{1,0:T(8,128)(2,1)S(1)}, u32[]{:S(2)}) copy-start(bf16[64,1024]{1,0:T(8,128)(2,1)S(1)} %collective-permute-done.10.refs_7_) | copy-start | bytes 393220
  34.7 12.2 %collective-permute-start.5 = (bf16[64,1024]{1,0:T(8,128)(2,1)}, bf16[64,1024]{1,0:T(8,128)(2,1)S(1)}, u32[]{:S(2)}, u32[]{:S(2)}) collective-permute-start(bf16[64,1024]{1,0:T(8,128)(2,1)} %bitcast.19), channel_id=1, source_target_pairs={{0,1},{1,0},{2,3},{3,2},{4,5},{5,4},{6,7},{7,6},{8,9},{9,8},{10,11... | collective-permute-start | bytes 393224 | tf_op jit(solution)/shard_map/ppermute | solution.py:14
  37.7 9.3 %copy-start.6 = (bf16[64,1024]{1,0:T(8,128)(2,1)}, bf16[64,1024]{1,0:T(8,128)(2,1)S(1)}, u32[]{:S(2)}) copy-start(bf16[64,1024]{1,0:T(8,128)(2,1)S(1)} %collective-permute-done.9.refs_6_) | copy-start | bytes 393220
  37.7 9.3 %copy-start.7 = (bf16[64,1024]{1,0:T(8,128)(2,1)}, bf16[64,1024]{1,0:T(8,128)(2,1)S(1)}, u32[]{:S(2)}) copy-start(bf16[64,1024]{1,0:T(8,128)(2,1)S(1)} %collective-permute-done.8.refs_5_) | copy-start | bytes 393220
  39.5 7.5 %copy-start.8 = (bf16[64,1024]{1,0:T(8,128)(2,1)}, bf16[64,1024]{1,0:T(8,128)(2,1)S(1)}, u32[]{:S(2)}) copy-start(bf16[64,1024]{1,0:T(8,128)(2,1)S(1)} %collective-permute-done.7.refs_3_) | copy-start | bytes 393220
  (2 other events, 1.4 us)
